TPU v7x, 32 devices: a whole 2x2x4 slice. The times are simulated.
32 devices in a mesh: group: 8 (over z, core), dev: 4 (over y, x).
Axes of the slice: x: 2, y: 2, z: 4, core: 2. Of those that a mesh axis runs over, the one named last changes fastest.
Arguments:
- tiles: bfloat16 [2304, 5, 128, 128], P(('group', 'dev')), may hold values from 0.00029945374 to 0.029907227
- tile_col: int32 [2304, 5], P(('group', 'dev')), may hold values from 0 to 15
- strip_group: int32 [2304], P(('group', 'dev')), may hold values from 0 to 7, as said below
- strip_slot: int32 [2304], P(('group', 'dev')), may hold values from 0 to 15
- live_count: int32 [32], P(('group', 'dev')), may hold values from 36 to 72, as said below
- omega: bfloat16 [16384, 128], P(('group', 'dev')), may hold values from -40 to 40
- idf: float32 [65536], P(('group', 'dev')), may hold values from 0.4 to 20
Outputs:
- q_basis: float32 [65536, 128], P(('group', 'dev'))
- doc_factor: bfloat16 [128, 16384], P(None, ('group', 'dev'))
Inputs may be any that keep to these rules, and one draw needn't show every extreme that they name: `strip_group`: among the 72 strips of one device at most 12 name one group; in every draw one group is named by exactly 12 strips of every device. `live_count`: some device has all 72 strips live.
All inputs are finite; a program needn't handle non-finite values.
Results may differ from a plain program's by a relative error of at most 0.0034.
Values may be sent and summed in bfloat16 or wider, within the bound.
No kernel may reach another device: no remote copies, remote signals or barrier semaphores. Data moves between devices by JAX's collectives and lax.ppermute only.
A program may use at most 128 MiB of HBM per device.

v0:
```python
import jax
import jax.numpy as jnp
from jax import lax
from jax.sharding import PartitionSpec as P


def on_device(tiles, tile_col, strip_group, strip_slot, live_count, omega, idf):
    n_group = lax.axis_size("group")
    n_dev = lax.axis_size("dev")
    strips = tiles.shape[0]
    tile_edge = tiles.shape[2]
    sketch_cols = omega.shape[1]
    owned_blocks = idf.shape[0] // tile_edge
    capacity = max(2, (4 * strips + 3 * n_group - 1) // (3 * n_group))
    alive_mask = (jnp.arange(strips) < live_count[0]).astype(jnp.float32)
    group_omega = lax.all_gather(omega, "dev", axis=0, tiled=True)
    omega_blocks = group_omega.reshape(-1, tile_edge, sketch_cols)
    picked = omega_blocks[tile_col]
    partial_value = jnp.einsum("stij,stjk->sik", tiles, picked, preferred_element_type=jnp.float32)
    partial_value = partial_value * alive_mask[:, None, None]
    member = (strip_group[:, None] == jnp.arange(n_group)[None, :]).astype(jnp.int32)
    rank_in = jnp.sum((jnp.cumsum(member, axis=0) - member) * member, axis=1)
    position = strip_group * capacity + rank_in
    labels = jnp.where(alive_mask > 0, strip_slot, -1).astype(jnp.float32)
    outgoing = (
        jnp.zeros((n_group * capacity, tile_edge, sketch_cols), jnp.float32)
        .at[position]
        .set(partial_value)
    )
    out_labels = jnp.full((n_group * capacity,), -1.0, jnp.float32).at[position].set(labels)
    arrived, arrived_labels = (
        lax.all_to_all(
            outgoing.reshape(n_group, capacity, tile_edge, sketch_cols),
            "group",
            split_axis=0,
            concat_axis=0,
            tiled=True,
        ),
        lax.all_to_all(
            out_labels.reshape(n_group, capacity), "group", split_axis=0, concat_axis=0, tiled=True
        ),
    )
    slot_ids = arrived_labels.reshape(-1).astype(jnp.int32)
    chooser = (jnp.arange(owned_blocks)[:, None] == slot_ids[None, :]).astype(jnp.float32)
    owned_rows = jnp.einsum(
        "rs,sik->rik",
        chooser,
        arrived.reshape(-1, tile_edge, sketch_cols),
        precision=lax.Precision.HIGHEST,
        preferred_element_type=jnp.float32,
    )
    sketch = owned_rows.reshape(-1, sketch_cols) * idf[:, None]
    total_terms = idf.shape[0] * n_group * n_dev
    local_gram = lax.dot_general(
        sketch,
        sketch,
        (((0,), (0,)), ((), ())),
        precision=lax.Precision.HIGHEST,
        preferred_element_type=jnp.float32,
    )
    gram_matrix = lax.psum(local_gram, ("group", "dev")) / total_terms
    lower_factor = jnp.linalg.cholesky(gram_matrix)
    q_basis = jax.scipy.linalg.solve_triangular(lower_factor, sketch.T, lower=True).T
    weighted = (
        (idf[:, None] * q_basis).astype(jnp.bfloat16).reshape(owned_blocks, tile_edge, sketch_cols)
    )
    band_rows = lax.all_gather(weighted, "group", axis=0, tiled=True)
    strip_q = band_rows[strip_group * owned_blocks + strip_slot]
    strip_q = strip_q * alive_mask.astype(jnp.bfloat16)[:, None, None]
    contrib = jnp.einsum("sik,stij->stkj", strip_q, tiles, preferred_element_type=jnp.float32)
    col_blocks = n_dev * (omega.shape[0] // tile_edge)
    doc_part = jax.ops.segment_sum(
        contrib.reshape(-1, sketch_cols, tile_edge), tile_col.reshape(-1), num_segments=col_blocks
    )
    my_docs = lax.psum_scatter(doc_part, "dev", scatter_dimension=0, tiled=True)
    doc_factor = jnp.transpose(my_docs, (1, 0, 2)).reshape(sketch_cols, -1).astype(jnp.bfloat16)
    return (q_basis, doc_factor)


def solution(mesh):
    placed = (
        P(("group", "dev"), None, None, None),
        P(("group", "dev"), None),
        P(("group", "dev")),
        P(("group", "dev")),
        P(("group", "dev")),
        P(("group", "dev"), None),
        P(("group", "dev")),
    )
    return jax.shard_map(
        on_device,
        mesh=mesh,
        in_specs=placed,
        out_specs=(P(("group", "dev"), None), P(None, ("group", "dev"))),
        check_vma=False,
    )
```

profile of v0, /device:TPU:0, one launch (start us, length us, event | category | flops | bytes accessed | tf_op | source)
XLA Modules:
  0.0 527.5 jit_solution(2830530185264732526)
XLA Ops:
  7.8 0.7 fusion.14
  8.7 0.8 select_reduce_fusion.1
  9.5 0.7 compare_select_fusion.1
  10.2 0.8 scatter_custom_fusion
  11.0 0.7 all_to_all.9
  11.7 6.4 %all-to-all-start = ((f32[8,1,12]{2,1,0:T(1,128)}), f32[8,1,12]{2,1,0:T(1,128)S(1)}, u32[]{:S(2)}, u32[]{:S(2)}) async-start(f32[8,1,12]{2,1,0:T(1,128)} %bitcast.1), calls=%async_computation | async-start | bytes 8192 | tf_op jit(solution)/shard_map/all_to_all | solution.py:39
  18.0 11.5 %all_gather.6 = bf16[2048,128]{1,0:T(8,128)(2,1)S(1)} all-gather(bf16[512,128]{1,0:T(8,128)(2,1)} %param.12), channel_id=1, replica_groups=mesh['group'=8,'dev'=4] {'dev'}, dimensions={0}, use_global_device_ids=true | all-gather | bytes 655360 | tf_op jit(solution)/shard_map/all_gather | solution.py:16
  29.5 0.7 compare_select_fusion
  30.5 11.1 %gather_fusion = bf16[360,128,128]{2,1,0:T(8,128)(2,1)} fusion(bf16[16,128,128]{2,1,0:T(8,128)(2,1)S(1)} %bitcast.53, s32[1024]{0:T(1024)S(1)} %pad_clamp_fusion.1), kind=kCustom, calls=%fused_computation | custom fusion | bytes 23594400 | tf_op jit(solution)/shard_map/gather | solution.py:18
  41.6 11.8 %fusion.2 = f32[72,128,128]{1,2,0:T(8,128)} fusion(f32[72]{0:T(128)S(1)} %compare_convert_fusion, bf16[72,5,128,128]{3,2,1,0:T(8,128)(2,1)} %bitcast.55, bf16[72,5,128,128]{3,2,1,0:T(8,128)(2,1)} %param.7), kind=kOutput, calls=%fused_computation.8 | convolution fusion | flops 1511129088 | bytes 28311840 | tf_op jit(solution)/shard_map/stij,stjk->sik/dot_general | solution.py:19
  53.3 6.1 %copy.43 = f32[72,128,128]{2,1,0:T(8,128)} copy(f32[72,128,128]{1,2,0:T(8,128)} %fusion.2) | data formatting | bytes 9437184 | tf_op jit(solution)/shard_map/mul | solution.py:20
  59.4 3.4 broadcast_in_dim.36
  62.9 14.4 %scatter_fusion = f32[96,128,128]{2,1,0:T(8,128)} fusion(f32[96,128,128]{2,1,0:T(8,128)} %broadcast_in_dim.36, s32[72]{0:T(128)S(1)} %get-tuple-element.7, f32[72,128,128]{2,1,0:T(8,128)} %copy.43), kind=kCustom, calls=%fused_computation.3 | custom fusion | bytes 14156064 | tf_op jit(solution)/shard_map/scatter | solution.py:28
  77.3 4.9 all-to-all-start.1
  82.6 138.5 %all-to-all-done.1 = f32[8,12,128,128]{3,2,1,0:T(8,128)} async-done(((f32[8,12,128,128]{3,2,1,0:T(8,128)}), f32[8,12,128,128]{3,2,1,0:T(8,128)}, u32[]{:S(2)}, u32[]{:S(2)}) %all-to-all-start.1) | async-done | bytes 6291488 | tf_op jit(solution)/shard_map/all_to_all | solution.py:32
  221.1 8.3 %fusion.6 = f32[16,128,128]{2,0,1:T(8,128)S(1)} fusion(f32[96,128,128]{2,1,0:T(8,128)} %bitcast.9, f32[16,128]{0,1:T(8,128)S(1)} %copy.45, s32[96]{0:T(128)S(1)} %convert_element_type.50), kind=kOutput, calls=%fused_computation.12 | convolution fusion | flops 302253568 | bytes 7348608 | tf_op jit(solution)/shard_map/rs,sik->rik/dot_general | solution.py:45
  229.4 2.4 convolution_bitcast_fusion
  232.5 116.9 %all-reduce.2.cloned.1.call-done = f32[128,128]{0,1:T(8,128)} async-done(((f32[128,128]{0,1:T(8,128)}), f32[128,128]{0,1:T(8,128)}) %all-reduce.2.cloned.1.call-update) | async-done | bytes 65552 | tf_op jit(solution)/shard_map/psum | solution.py:61
  349.4 0.8 broadcast_multiply_fusion
  350.4 0.9 fusion.13
  351.2 11.7 %cholesky.16 = f32[128,128]{1,0:T(8,128)S(1)} custom-call(f32[128,128]{1,0:T(8,128)S(1)} %fusion.13), custom_call_target="Cholesky" | custom-call | tf_op jit(solution)/shard_map/jit(cholesky)/cholesky | solution.py:62
  363.6 0.7 fusion.10
  364.3 9.8 %custom-call.7 = f32[1,128,128]{1,2,0:T(8,128)S(1)} custom-call(f32[1,128,128]{2,1,0:T(8,128)S(1)} %fusion.10), custom_call_target="InvertDiagBlocksLowerTriangular" | custom-call | tf_op jit(solution)/shard_map/jit(_solve_triangular)/triangular_solve | solution.py:63
  374.1 2.1 multiply_convert_fusion
  376.8 47.7 %all-gather.2.cloned.1.call-done = bf16[128,128,128]{2,1,0:T(8,128)(2,1)} async-done(((bf16[16,128,128]{2,1,0:T(8,128)(2,1)}), bf16[128,128,128]{2,1,0:T(8,128)(2,1)}) %all-gather.2.cloned.1.call-update) | async-done | bytes 4194320 | tf_op jit(solution)/shard_map/all_gather | solution.py:67
  424.5 3.2 gather_fusion.1
  427.7 15.5 %fusion.3 = f32[72,128,5,128]{3,1,2,0:T(8,128)} fusion(bf16[72,5,128,128]{3,2,1,0:T(8,128)(2,1)} %param.7, bf16[72,128,128]{2,1,0:T(8,128)(2,1)S(1)} %gather_fusion.1, bf16[72]{0:T(256)(128)(2,1)S(1)} %fusion.21), kind=kOutput, calls=%fused_computation.9 | convolution fusion | flops 1514668032 | bytes 37748880 | tf_op jit(solution)/shard_map/sik,stij->stkj/dot_general | solution.py:70
  443.3 47.9 %scatter_fusion.1 = f32[16,128,128]{2,1,0:T(8,128)S(1)} fusion(f32[16,128,128]{2,1,0:T(8,128)S(1)} %broadcast_in_dim.38, s32[360]{0:T(512)S(1)} %reshape.109, f32[360,128,128]{2,1,0:T(8,128)} %bitcast.54), kind=kCustom, calls=%fused_computation.4 | custom fusion | flops 5898240 | bytes 70780320 | tf_op jit(solution)/shard_map/scatter-add | solution.py:72
  491.2 1.0 copy-done
  492.2 26.9 %reduce-scatter.2.cloned.1.call-done = f32[4,128,128]{2,1,0:T(8,128)} async-done(((f32[16,128,128]{2,1,0:T(8,128)}), f32[4,128,128]{2,1,0:T(8,128)}) %reduce-scatter.2.cloned.1.call-update) | async-done | bytes 262160 | tf_op jit(solution)/shard_map/reduce_scatter | solution.py:75
  519.1 1.0 convert_bitcast_fusion
  520.2 0.8 copy.52
  (30 shorter events, 3.0 us)
Async XLA Ops:
  11.7 65.6 %all-to-all-start = ((f32[8,1,12]{2,1,0:T(1,128)}), f32[8,1,12]{2,1,0:T(1,128)S(1)}, u32[]{:S(2)}, u32[]{:S(2)}) async-start(f32[8,1,12]{2,1,0:T(1,128)} %bitcast.1), calls=%async_computation | async-start | bytes 8192 | tf_op jit(solution)/shard_map/all_to_all | solution.py:39
  77.3 5.1 copy-start.1
  77.3 143.8 %all-to-all-start.1 = ((f32[8,12,128,128]{3,2,1,0:T(8,128)}), f32[8,12,128,128]{3,2,1,0:T(8,128)}, u32[]{:S(2)}, u32[]{:S(2)}) async-start(f32[8,12,128,128]{3,2,1,0:T(8,128)} %bitcast.56), calls=%async_computation.1 | async-start | bytes 12582912 | tf_op jit(solution)/shard_map/all_to_all | solution.py:32
  82.2 267.2 %all-reduce.2.cloned.1.call-start = ((), (), s32[]{:S(2)}) async-start(), calls=%async_computation.3 | async-start | bytes 131072 | tf_op jit(solution)/shard_map/psum | solution.py:61
  221.1 155.4 %copy-start.2 = (s32[72,5]{0,1:T(8,128)S(1)}, s32[72,5]{0,1:T(8,128)}, u32[]{:S(2)}) copy-start(s32[72,5]{0,1:T(8,128)} %param.8) | copy-start | bytes 4324
  231.9 192.6 %all-gather.2.cloned.1.call-start = ((), (), s32[]{:S(2)}) async-start(), calls=%async_computation.4 | async-start | bytes 4718592 | tf_op jit(solution)/shard_map/all_gather | solution.py:67
  376.2 142.9 %reduce-scatter.2.cloned.1.call-start = ((), (), s32[]{:S(2)}) async-start(), calls=%async_computation.5 | async-start | bytes 1310720 | tf_op jit(solution)/shard_map/reduce_scatter | solution.py:75
  491.2 1.0 copy-start
Sparse Core Ops, SparseCore 0:
  232.0 117.3 all-reduce.1
  376.4 48.1 all-gather.1
  492.3 26.7 reduce-scatter.1
where the time goes:
time: 529 us; the launch traced here: 528 us
  waiting for transfers between devices  330 us (62%)
  other arithmetic  76.5 us (14%)
  local copies, waits for them, and re-layouts  42.8 us (8%)
  matrix products  40.1 us (8%)
  between operations  14.6 us (3%)
  starting transfers between devices  12 us (2%)
  blocking collectives  11.5 us (2%)
    all_to_all x1, waiting for transfers between devices, on_device(): lax.all_to_all(outgoing.reshape(n_group, capacity, tile_edge, sketch_cols...  138 us
    psum x1, waiting for transfers between devices, on_device(): gram_matrix = lax.psum(local_gram, ('group', 'dev')) / total_terms  117 us
    scatter-add x1, other arithmetic, on_device(): jax.ops.segment_sum(contrib.reshape(-1, sketch_cols, tile_edge), tile_col...  47.9 us
    all_gather x1, waiting for transfers between devices, on_device(): band_rows = lax.all_gather(weighted, 'group', axis=0, tiled=True)  47.7 us
    reduce_scatter x1, waiting for transfers between devices, on_device(): my_docs = lax.psum_scatter(doc_part, 'dev', scatter_dimension=0, tiled=True)  26.9 us
    dot_general x1, matrix products, on_device(): jnp.einsum('sik,stij->stkj', strip_q, tiles, preferred_element_type=jnp.f...  15.5 us
    scatter x1, local copies, waits for them, and re-layouts, on_device(): outgoing = jnp.zeros((n_group * capacity, tile_edge, sketch_cols), jnp.fl...  14.4 us
    another operation x3, other arithmetic, on_device(): lower_factor = jnp.linalg.cholesky(gram_matrix)  12.4 us
  transfers between devices with their start and end apart: 5, of which 4 were waited for; matrix products, arithmetic and copies ran while one was open for 9% of the time, Pallas kernels for 0%

commit v1 on v0

--- a/solution.py
+++ b/solution.py
@@ -58,7 +58,7 @@
         precision=lax.Precision.HIGHEST,
         preferred_element_type=jnp.float32,
     )
-    gram_matrix = lax.psum(local_gram, ("group", "dev")) / total_terms
+    gram_matrix = lax.psum(lax.psum(local_gram, "dev"), "group") / total_terms
     lower_factor = jnp.linalg.cholesky(gram_matrix)
     q_basis = jax.scipy.linalg.solve_triangular(lower_factor, sketch.T, lower=True).T
     weighted = (

time: 529 us -> 507 us (0.958)
  waiting for transfers between devices: 330 us -> 307 us
    psum x1 -> x2, waiting for transfers between devices: 117 us -> 96.3 us  [on_device(): gram_matrix = lax.psum(lax.psum(local_gram, 'dev'), 'group') / total_terms]
  transfers between devices with their start and end apart: 5 -> 6, of which waited for: 4 -> 5; matrix products, arithmetic and copies ran while one was open for 9% -> 10% of each run, Pallas kernels for 0% -> 0%
where the time goes in v1:
time: 507 us; the launch traced here: 505 us
  waiting for transfers between devices  307 us (61%)
  other arithmetic  76.5 us (15%)
  local copies, waits for them, and re-layouts  42.8 us (8%)
  matrix products  40.1 us (8%)
  between operations  14.6 us (3%)
  starting transfers between devices  12.1 us (2%)
  blocking collectives  11.5 us (2%)
    all_to_all x1, waiting for transfers between devices, on_device(): lax.all_to_all(outgoing.reshape(n_group, capacity, tile_edge, sketch_cols...  138 us
    psum x2, waiting for transfers between devices, on_device(): gram_matrix = lax.psum(lax.psum(local_gram, 'dev'), 'group') / total_terms  96.3 us
    scatter-add x1, other arithmetic, on_device(): jax.ops.segment_sum(contrib.reshape(-1, sketch_cols, tile_edge), tile_col...  47.9 us
    all_gather x1, waiting for transfers between devices, on_device(): band_rows = lax.all_gather(weighted, 'group', axis=0, tiled=True)  45.5 us
    reduce_scatter x1, waiting for transfers between devices, on_device(): my_docs = lax.psum_scatter(doc_part, 'dev', scatter_dimension=0, tiled=True)  26.9 us
    dot_general x1, matrix products, on_device(): jnp.einsum('sik,stij->stkj', strip_q, tiles, preferred_element_type=jnp.f...  15.5 us
    scatter x1, local copies, waits for them, and re-layouts, on_device(): outgoing = jnp.zeros((n_group * capacity, tile_edge, sketch_cols), jnp.fl...  14.4 us
    another operation x3, other arithmetic, on_device(): lower_factor = jnp.linalg.cholesky(gram_matrix)  12.4 us
  transfers between devices with their start and end apart: 6, of which 5 were waited for; matrix products, arithmetic and copies ran while one was open for 10% of the time, Pallas kernels for 0%

profile of v1, /device:TPU:0, one launch (start us, length us, event | category | flops | bytes accessed | tf_op | source)
XLA Modules:
  0.0 504.8 jit_solution(2964049566211567149)
XLA Ops:
  7.8 0.7 fusion.14
  8.7 0.8 select_reduce_fusion.1
  9.5 0.7 compare_select_fusion.1
  10.2 0.8 scatter_custom_fusion
  11.0 0.7 all_to_all.9
  11.7 6.4 %all-to-all-start = ((f32[8,1,12]{2,1,0:T(1,128)}), f32[8,1,12]{2,1,0:T(1,128)S(1)}, u32[]{:S(2)}, u32[]{:S(2)}) async-start(f32[8,1,12]{2,1,0:T(1,128)} %bitcast.1), calls=%async_computation | async-start | bytes 8192 | tf_op jit(solution)/shard_map/all_to_all | solution.py:39
  18.0 11.5 %all_gather.6 = bf16[2048,128]{1,0:T(8,128)(2,1)S(1)} all-gather(bf16[512,128]{1,0:T(8,128)(2,1)} %param.12), channel_id=1, replica_groups=mesh['group'=8,'dev'=4] {'dev'}, dimensions={0}, use_global_device_ids=true | all-gather | bytes 655360 | tf_op jit(solution)/shard_map/all_gather | solution.py:16
  29.5 0.7 compare_select_fusion
  30.5 11.1 %gather_fusion = bf16[360,128,128]{2,1,0:T(8,128)(2,1)} fusion(bf16[16,128,128]{2,1,0:T(8,128)(2,1)S(1)} %bitcast.53, s32[1024]{0:T(1024)S(1)} %pad_clamp_fusion.1), kind=kCustom, calls=%fused_computation | custom fusion | bytes 23594400 | tf_op jit(solution)/shard_map/gather | solution.py:18
  41.6 11.8 %fusion.2 = f32[72,128,128]{1,2,0:T(8,128)} fusion(f32[72]{0:T(128)S(1)} %compare_convert_fusion, bf16[72,5,128,128]{3,2,1,0:T(8,128)(2,1)} %bitcast.55, bf16[72,5,128,128]{3,2,1,0:T(8,128)(2,1)} %param.7), kind=kOutput, calls=%fused_computation.8 | convolution fusion | flops 1511129088 | bytes 28311840 | tf_op jit(solution)/shard_map/stij,stjk->sik/dot_general | solution.py:19
  53.3 6.1 %copy.43 = f32[72,128,128]{2,1,0:T(8,128)} copy(f32[72,128,128]{1,2,0:T(8,128)} %fusion.2) | data formatting | bytes 9437184 | tf_op jit(solution)/shard_map/mul | solution.py:20
  59.4 3.4 broadcast_in_dim.36
  62.9 14.4 %scatter_fusion = f32[96,128,128]{2,1,0:T(8,128)} fusion(f32[96,128,128]{2,1,0:T(8,128)} %broadcast_in_dim.36, s32[72]{0:T(128)S(1)} %get-tuple-element.7, f32[72,128,128]{2,1,0:T(8,128)} %copy.43), kind=kCustom, calls=%fused_computation.3 | custom fusion | bytes 14156064 | tf_op jit(solution)/shard_map/scatter | solution.py:28
  77.3 4.9 all-to-all-start.1
  82.6 138.5 %all-to-all-done.1 = f32[8,12,128,128]{3,2,1,0:T(8,128)} async-done(((f32[8,12,128,128]{3,2,1,0:T(8,128)}), f32[8,12,128,128]{3,2,1,0:T(8,128)}, u32[]{:S(2)}, u32[]{:S(2)}) %all-to-all-start.1) | async-done | bytes 6291488 | tf_op jit(solution)/shard_map/all_to_all | solution.py:32
  221.1 8.3 %fusion.6 = f32[16,128,128]{2,0,1:T(8,128)S(1)} fusion(f32[96,128,128]{2,1,0:T(8,128)} %bitcast.9, f32[16,128]{0,1:T(8,128)S(1)} %copy.45, s32[96]{0:T(128)S(1)} %convert_element_type.50), kind=kOutput, calls=%fused_computation.12 | convolution fusion | flops 302253568 | bytes 7348608 | tf_op jit(solution)/shard_map/rs,sik->rik/dot_general | solution.py:45
  229.4 2.4 convolution_bitcast_fusion
  232.0 39.9 %all-reduce.3.cloned.1.call-done = f32[128,128]{0,1:T(8,128)} async-done(((f32[128,128]{0,1:T(8,128)}), f32[128,128]{0,1:T(8,128)}) %all-reduce.3.cloned.1.call-update) | async-done | bytes 65552 | tf_op jit(solution)/shard_map/psum | solution.py:61
  272.5 56.4 %all-reduce.5.cloned.1.call-done = f32[128,128]{0,1:T(8,128)} async-done(((f32[128,128]{0,1:T(8,128)}), f32[128,128]{0,1:T(8,128)}) %all-reduce.5.cloned.1.call-update) | async-done | bytes 65552 | tf_op jit(solution)/shard_map/psum | solution.py:61
  328.9 0.8 broadcast_multiply_fusion
  329.9 0.9 fusion.13
  330.7 11.7 %cholesky.16 = f32[128,128]{1,0:T(8,128)S(1)} custom-call(f32[128,128]{1,0:T(8,128)S(1)} %fusion.13), custom_call_target="Cholesky" | custom-call | tf_op jit(solution)/shard_map/jit(cholesky)/cholesky | solution.py:62
  343.8 9.8 %custom-call.7 = f32[1,128,128]{1,2,0:T(8,128)S(1)} custom-call(f32[1,128,128]{2,1,0:T(8,128)S(1)} %fusion.10), custom_call_target="InvertDiagBlocksLowerTriangular" | custom-call | tf_op jit(solution)/shard_map/jit(_solve_triangular)/triangular_solve | solution.py:63
  353.6 2.1 multiply_convert_fusion
  356.3 45.5 %all-gather.2.cloned.1.call-done = bf16[128,128,128]{2,1,0:T(8,128)(2,1)} async-done(((bf16[16,128,128]{2,1,0:T(8,128)(2,1)}), bf16[128,128,128]{2,1,0:T(8,128)(2,1)}) %all-gather.2.cloned.1.call-update) | async-done | bytes 4194320 | tf_op jit(solution)/shard_map/all_gather | solution.py:67
  401.8 3.2 gather_fusion.1
  405.0 15.5 %fusion.3 = f32[72,128,5,128]{3,1,2,0:T(8,128)} fusion(bf16[72,5,128,128]{3,2,1,0:T(8,128)(2,1)} %param.7, bf16[72,128,128]{2,1,0:T(8,128)(2,1)S(1)} %gather_fusion.1, bf16[72]{0:T(256)(128)(2,1)S(1)} %fusion.21), kind=kOutput, calls=%fused_computation.9 | convolution fusion | flops 1514668032 | bytes 37748880 | tf_op jit(solution)/shard_map/sik,stij->stkj/dot_general | solution.py:70
  420.6 47.9 %scatter_fusion.1 = f32[16,128,128]{2,1,0:T(8,128)S(1)} fusion(f32[16,128,128]{2,1,0:T(8,128)S(1)} %broadcast_in_dim.38, s32[360]{0:T(512)S(1)} %reshape.109, f32[360,128,128]{2,1,0:T(8,128)} %bitcast.54), kind=kCustom, calls=%fused_computation.4 | custom fusion | flops 5898240 | bytes 70780320 | tf_op jit(solution)/shard_map/scatter-add | solution.py:72
  468.5 1.0 copy-done
  469.5 26.9 %reduce-scatter.2.cloned.1.call-done = f32[4,128,128]{2,1,0:T(8,128)} async-done(((f32[16,128,128]{2,1,0:T(8,128)}), f32[4,128,128]{2,1,0:T(8,128)}) %reduce-scatter.2.cloned.1.call-update) | async-done | bytes 262160 | tf_op jit(solution)/shard_map/reduce_scatter | solution.py:75
  496.4 1.0 convert_bitcast_fusion
  497.5 0.8 copy.52
  (33 shorter events, 3.7 us)
Async XLA Ops:
  11.7 65.6 %all-to-all-start = ((f32[8,1,12]{2,1,0:T(1,128)}), f32[8,1,12]{2,1,0:T(1,128)S(1)}, u32[]{:S(2)}, u32[]{:S(2)}) async-start(f32[8,1,12]{2,1,0:T(1,128)} %bitcast.1), calls=%async_computation | async-start | bytes 8192 | tf_op jit(solution)/shard_map/all_to_all | solution.py:39
  77.3 5.1 %copy-start.1 = (f32[2048]{0:T(1024)S(1)}, f32[2048]{0:T(1024)}, u32[]{:S(2)}) copy-start(f32[2048]{0:T(1024)} %param.13) | copy-start | bytes 24580
  77.3 143.8 %all-to-all-start.1 = ((f32[8,12,128,128]{3,2,1,0:T(8,128)}), f32[8,12,128,128]{3,2,1,0:T(8,128)}, u32[]{:S(2)}, u32[]{:S(2)}) async-start(f32[8,12,128,128]{3,2,1,0:T(8,128)} %bitcast.56), calls=%async_computation.1 | async-start | bytes 12582912 | tf_op jit(solution)/shard_map/all_to_all | solution.py:32
  82.2 189.7 %all-reduce.3.cloned.1.call-start = ((), (), s32[]{:S(2)}) async-start(), calls=%async_computation.3 | async-start | bytes 131072 | tf_op jit(solution)/shard_map/psum | solution.py:61
  221.1 134.9 %copy-start.2 = (s32[72,5]{0,1:T(8,128)S(1)}, s32[72,5]{0,1:T(8,128)}, u32[]{:S(2)}) copy-start(s32[72,5]{0,1:T(8,128)} %param.8) | copy-start | bytes 4324
  231.9 97.0 %all-reduce.5.cloned.1.call-start = ((), (), s32[]{:S(2)}) async-start(), calls=%async_computation.4 | async-start | bytes 131072 | tf_op jit(solution)/shard_map/psum | solution.py:61
  271.9 129.9 %all-gather.2.cloned.1.call-start = ((), (), s32[]{:S(2)}) async-start(), calls=%async_computation.5 | async-start | bytes 4718592 | tf_op jit(solution)/shard_map/all_gather | solution.py:67
  355.7 140.7 %reduce-scatter.2.cloned.1.call-start = ((), (), s32[]{:S(2)}) async-start(), calls=%async_computation.6 | async-start | bytes 1310720 | tf_op jit(solution)/shard_map/reduce_scatter | solution.py:75
  468.5 1.0 copy-start
Sparse Core Ops, SparseCore 0:
  232.0 39.8 all-reduce.2
  274.2 54.6 all-reduce.4
  355.9 45.9 all-gather.1
  469.6 26.7 reduce-scatter.1
